TPU v7x, 256 devices: a whole 4x4x8 slice. The times are simulated.
256 devices in a mesh: outer: 16 (over x, z_hi), inner: 16 (over z_lo, y, core).
Axes of the slice: x: 4, y: 4, z: 8 (z_hi: 4, z_lo: 2; z = z_hi * 2 + z_lo), core: 2. Of those that a mesh axis runs over, the one named last changes fastest.
Arguments:
- query_in: bfloat16 [32768, 1024], P(('outer', 'inner')), may hold values from -6 to 6
- key_in: bfloat16 [32768, 1024], P(('outer', 'inner')), may hold values from -6 to 6
- value_in: bfloat16 [32768, 1024], P(('outer', 'inner')), may hold values from -6 to 6
- conv_taps: float32 [3, 3, 1024], replicated, may hold values from -3.5 to 3.5
- long_filter: float32 [32768, 1024], P(('outer', 'inner')), may hold values from -1.1 to 1.1
- skip_gain: float32 [1024], replicated, may hold values from 0.5 to 1.5
- grad_out: bfloat16 [32768, 1024], P(('outer', 'inner')), may hold values from -6 to 6
Outputs:
- output: bfloat16 [32768, 1024], P(('outer', 'inner'))
- grad_query: bfloat16 [32768, 1024], P(('outer', 'inner'))
- grad_key: bfloat16 [32768, 1024], P(('outer', 'inner'))
- grad_value: bfloat16 [32768, 1024], P(('outer', 'inner'))
All inputs are finite; a program needn't handle non-finite values.
Results may differ from a plain program's by a relative error of at most 0.001.
Values may be sent and summed in bfloat16 or wider, within the bound.
A program may use at most 64 MiB of HBM per device.

v0:
```python
import functools

import jax
import jax.numpy as jnp
import numpy as np
from jax import lax
from jax.experimental import pallas as pl
from jax.experimental.pallas import tpu as pltpu
from jax.sharding import PartitionSpec as P

MESH = pl.DeviceIdType.MESH
F32, BF16 = jnp.float32, jnp.bfloat16
X, Z, Y, C = 4, 8, 4, 2
W = X * Y * C
D = 256
T = 128
POINTS = 2 * D * T


def dft_constants():
    k = np.arange(D)[:, None] + 0.5
    d = np.arange(D)[None, :]
    coarse = 2 * np.pi * (k * d / (2 * D) % 1.0)
    forward = np.concatenate([np.cos(coarse), -np.sin(coarse)], 0)
    backward = np.concatenate([np.cos(coarse).T, -np.sin(coarse).T], 1) * (2.0 / POINTS)
    t = np.arange(T)[None, :]
    turn = 2 * np.pi * (k * t / POINTS % 1.0)
    fine = 2 * np.pi * (t.T * t % T) / T
    c, s = np.cos(fine), np.sin(fine)
    fine_forward = np.block([[c, -s], [s, c]])
    fine_backward = np.block([[c, s], [-s, c]])

    def halves(m):
        m = m.astype(np.float32)
        high = m.astype(jnp.bfloat16)
        low = (m - high.astype(np.float32)).astype(jnp.bfloat16)
        return np.stack([high, low])

    fine_both = np.stack([halves(fine_forward), halves(fine_backward)])
    twist = np.stack([np.cos(turn), np.sin(turn)]).astype(np.float32)
    return halves(forward), halves(backward), fine_both, twist


def place():
    o, i = lax.axis_index("outer"), lax.axis_index("inner")
    return o // 4, (o % 4) * 2 + i // 8, i % 8


def device(x, z, yc):
    return (x * 4 + z // 2, (z % 2) * 8 + yc)


def halves_of(v):
    high = v.astype(BF16)
    return high, (v - high.astype(F32)).astype(BF16)


def dot(a, b):
    return jnp.dot(a, b, preferred_element_type=F32)


def choose_matrix():
    r = lax.broadcasted_iota(jnp.int32, (256, 256), 0)
    c = lax.broadcasted_iota(jnp.int32, (256, 256), 1)
    wanted = ((r // 4) % 2) * 128 + (r // 8) * 4 + r % 4
    return jnp.where(c == wanted, 1.0, 0.0).astype(BF16)


def main_kernel(
    q_hbm, k_hbm, v_hbm, g_hbm, f_hbm, taps, skip, fwd_hbm, bwd_hbm, fine_hbm, twist_hbm,
    back,
    kin, vin, qin, gin, fin, fwd, bwd, fine, twist,
    choose, snd, mid, rcv, rows, spec, coarse, work, gated, mixed, grad, streams, osnd, omid,
    in_sem, local_sem, zs_sem, zr_sem, xs_sem, xr_sem,
):
    x, z, yc = place()
    w = x * 8 + yc

    loads = [
        pltpu.make_async_copy(a, b, in_sem.at[n])
        for n, (a, b) in enumerate(
            [(f_hbm, fin), (k_hbm, kin), (v_hbm, vin), (q_hbm, qin), (g_hbm, gin),
             (fwd_hbm, fwd), (fine_hbm, fine), (twist_hbm, twist), (bwd_hbm, bwd)]
        )
    ]
    for load in loads:
        load.start()

    barrier = pltpu.get_barrier_semaphore()

    def greet_z(i, _):
        pl.semaphore_signal(barrier, inc=1, device_id=device(x, (z + i) % Z, yc), device_id_type=MESH)
        return 0

    def greet_w(i, _):
        there = (w + i) % W
        pl.semaphore_signal(barrier, inc=1, device_id=device(there // 8, z, there % 8), device_id_type=MESH)
        return 0

    lax.fori_loop(1, Z, greet_z, 0)
    lax.fori_loop(1, W, greet_w, 0)
    choose[...] = choose_matrix()

    def pack(p, left, right):
        def block(b, _):
            cols = pl.ds(pl.multiple_of(b * 128, 128), 128)
            pair = jnp.concatenate([left(cols), right(cols)], axis=1)
            turned = lax.dot_general(
                choose[...], pair, (((1,), (1,)), ((), ())), preferred_element_type=F32
            )
            snd[p, b] = turned.reshape(W, 8, T).astype(BF16)
            return 0

        lax.fori_loop(0, Z, block, 0)

    def send_z(p, source, target):
        def one(i, _):
            s, dz = i // 7, i % 7 + 1
            zt = (z + dz) % Z
            pltpu.make_async_remote_copy(
                src_ref=source(zt, s), dst_ref=target(s),
                send_sem=zs_sem.at[p], recv_sem=zr_sem.at[p, s],
                device_id=device(x, zt, yc), device_id_type=MESH,
            ).start()
            return 0

        lax.fori_loop(0, X * (Z - 1), one, 0)
        for s in range(X):
            pltpu.make_async_copy(source(z, s), target(s), local_sem.at[p, s]).start()

    def forward(p, s, middle, target, own):
        part = middle.at[pl.ds(s * 8, 8), z]
        pltpu.make_async_copy(part, part, local_sem.at[p, s]).wait()
        arrived = middle.at[pl.ds(s * 8, 8), pl.ds(0, Z - 1)]
        pltpu.make_async_remote_copy(
            src_ref=arrived, dst_ref=arrived, send_sem=zs_sem.at[p], recv_sem=zr_sem.at[p, s],
            device_id=device(x, z, yc), device_id_type=MESH,
        ).wait_recv()

        def one(i, _):
            there = (yc + i) % 8
            @pl.when(jnp.logical_or(s != x, i != 0))
            def _():
                pltpu.make_async_remote_copy(
                    src_ref=middle.at[s * 8 + there], dst_ref=target,
                    send_sem=xs_sem.at[p], recv_sem=xr_sem.at[p],
                    device_id=device(s, z, there), device_id_type=MESH,
                ).start()
            return 0

        lax.fori_loop(0, 8, one, 0)

    def await_all(p, middle, target):
        own = pltpu.make_async_copy(middle.at[w], target, local_sem.at[p, X])
        own.start()
        own.wait()
        part = middle.at[pl.ds(0, W - 1)]
        pltpu.make_async_remote_copy(
            src_ref=part, dst_ref=part, send_sem=xs_sem.at[p], recv_sem=xr_sem.at[p],
            device_id=device(x, z, yc), device_id_type=MESH,
        ).wait_recv()

    def in_target(p):
        return rcv.at[p, x, :, yc]

    def in_send(p):
        send_z(
            p,
            lambda zt, s: snd.at[p, zt, pl.ds(s * 8, 8)],
            lambda s: mid.at[p, pl.ds(s * 8, 8), z],
        )

    def in_forward(p, s):
        forward(p, s, mid.at[p], in_target(p), None)

    def in_await(p):
        await_all(p, mid.at[p], in_target(p))
        for b in range(X):
            rows[pl.ds(b * 512, 512)] = rcv[p, b].astype(F32).reshape(512, T)

    def row(r):
        return rows[pl.ds(r, D, stride=8), :]

    loads[0].wait()

    def filter_high(cols):
        return fin[:, cols].astype(BF16)

    def filter_low(cols):
        value = fin[:, cols]
        return (value - value.astype(BF16).astype(F32)).astype(BF16)

    pack(0, filter_high, filter_low)
    pl.semaphore_wait(barrier, Z + W - 2)
    in_send(0)
    loads[1].wait()
    loads[2].wait()
    pack(1, lambda cols: kin[:, cols], lambda cols: vin[:, cols])
    in_send(1)
    loads[3].wait()
    loads[4].wait()
    pack(2, lambda cols: qin[:, cols], lambda cols: gin[:, cols])
    in_send(2)
    for load in loads[5:]:
        load.wait()

    lane = lax.broadcasted_iota(jnp.int32, (D, T), 1)
    block_row = lax.broadcasted_iota(jnp.int32, (D, T), 0)

    def delayed(v, n):
        turned = pltpu.roll(v, n, axis=1)
        before = jnp.where(block_row == 0, 0.0, pltpu.roll(turned, 1, axis=0))
        return jnp.where(lane < n, before, turned)

    def advanced(v, n):
        turned = pltpu.roll(v, T - n, axis=1)
        after = jnp.where(block_row == D - 1, 0.0, pltpu.roll(turned, D - 1, axis=0))
        return jnp.where(lane >= T - n, after, turned)

    first_channel = 4 * (z * W + w)

    def short_forward(v, stream, j):
        tap = [taps[stream, n, first_channel + j] for n in range(3)]
        return tap[0] * v + tap[1] * delayed(v, 1) + tap[2] * delayed(v, 2)

    def short_backward(v, stream, j):
        tap = [taps[stream, n, first_channel + j] for n in range(3)]
        return tap[0] * v + tap[1] * advanced(v, 1) + tap[2] * advanced(v, 2)

    def put_columns(v, at):
        high, low = halves_of(v)
        work[0, 0:D, pl.ds(at * T, T)] = high
        work[1, 0:D, pl.ds(at * T, T)] = low

    def transform(out, pair):
        for b in range(2):
            part = pl.ds(b * D, D)
            high = work[0, 0:D]
            coarse[part] = (
                dot(fwd[0, part], high) + dot(fwd[1, part], high) + dot(fwd[0, part], work[1, 0:D])
            )
        tc, ts = twist[0], twist[1]
        for n in range(2):
            cols = pl.ds(n * T, T)
            re, im = coarse[0:D, cols], coarse[D : 2 * D, cols]
            both = jnp.concatenate([re * tc + im * ts, im * tc - re * ts], axis=1)
            high, low = halves_of(both)
            out[2 * pair + n] = (
                dot(high, fine[0, 0]) + dot(low, fine[0, 0]) + dot(high, fine[0, 1])
            )

    def untransform(left, right, conjugate, out, pair):
        tc, ts = twist[0], twist[1]
        for n in range(2):
            a, b = left[2 * pair + n], right[2 * pair + n]
            ar, ai, br, bi = a[:, 0:T], a[:, T:], b[:, 0:T], b[:, T:]
            if conjugate:
                re, im = ar * br + ai * bi, ar * bi - ai * br
            else:
                re, im = ar * br - ai * bi, ar * bi + ai * br
            high, low = halves_of(jnp.concatenate([re, im], axis=1))
            back_spec = dot(high, fine[1, 0]) + dot(low, fine[1, 0]) + dot(high, fine[1, 1])
            gr, gi = back_spec[:, 0:T], back_spec[:, T:]
            cols = pl.ds(n * T, T)
            high, low = halves_of(gr * tc - gi * ts)
            work[0, 0:D, cols] = high
            work[1, 0:D, cols] = low
            high, low = halves_of(gi * tc + gr * ts)
            work[0, D : 2 * D, cols] = high
            work[1, D : 2 * D, cols] = low
        result = dot(bwd[0], work[0]) + dot(bwd[1], work[0]) + dot(bwd[0], work[1])
        for n in range(2):
            out[2 * pair + n] = result[:, n * T : n * T + T]

    for s in range(X):
        in_forward(0, s)
    in_await(0)

    def filter_pair(pair, _):
        in_forward(1, pair)
        for n in range(2):
            work[0, 0:D, pl.ds(n * T, T)] = row(2 * pair + n).astype(BF16)
            work[1, 0:D, pl.ds(n * T, T)] = row(2 * pair + n + 4).astype(BF16)
        transform(spec.at[0], pair)
        return 0

    lax.fori_loop(0, 2, filter_pair, 0)
    in_forward(1, 2)
    in_forward(1, 3)
    in_await(1)

    def gated_pair(pair, _):
        in_forward(2, pair)
        for n in range(2):
            j = 2 * pair + n
            short_k = short_forward(row(j), 1, j)
            short_v = short_forward(row(j + 4), 2, j)
            streams[0, j] = short_k
            streams[1, j] = short_v
            value = short_k * short_v
            gated[j] = value
            put_columns(value, n)
        transform(spec.at[1], pair)
        untransform(spec.at[1], spec.at[0], False, mixed, pair)
        for n in range(2):
            j = 2 * pair + n
            mixed[j] = mixed[j] + skip[first_channel + j] * gated[j]
        return 0

    lax.fori_loop(0, 2, gated_pair, 0)
    in_forward(2, 2)
    in_forward(2, 3)
    in_await(2)

    def query_channel(j, _):
        short_q = short_forward(row(j), 0, j)
        upstream = row(j + 4)
        grad[j] = upstream * short_q
        rows[pl.ds(j, D, stride=8), :] = short_q * mixed[j]
        rows[pl.ds(j + 4, D, stride=8), :] = short_backward(upstream * mixed[j], 0, j)
        return 0

    lax.fori_loop(0, 4, query_channel, 0)

    def out_send(p):
        for b in range(X):
            osnd[p, b] = rows[pl.ds(b * 512, 512)].reshape(Z, 8, 8, T).astype(BF16)
        send_z(
            p + 3,
            lambda zt, s: osnd.at[p, s, zt],
            lambda s: omid.at[p, pl.ds(s * 8, 8), z],
        )

    def out_target(p):
        return back.at[p, :, w]

    def out_forward(p, s):
        forward(p + 3, s, omid.at[p], out_target(p), None)

    out_send(0)

    def grad_pair(pair, _):
        for n in range(2):
            put_columns(grad[2 * pair + n], n)
        transform(spec.at[1], pair)
        out_forward(0, 2 * pair)
        untransform(spec.at[0], spec.at[1], True, mixed, pair)
        for n in range(2):
            j = 2 * pair + n
            total = mixed[j] + skip[first_channel + j] * grad[j]
            rows[pl.ds(j, D, stride=8), :] = short_backward(total * streams[1, j], 1, j)
            rows[pl.ds(j + 4, D, stride=8), :] = short_backward(total * streams[0, j], 2, j)
        out_forward(0, 2 * pair + 1)
        return 0

    lax.fori_loop(0, 2, grad_pair, 0)
    out_send(1)
    for s in range(X):
        out_forward(1, s)
    for p in range(2):
        await_all(p + 3, omid.at[p], out_target(p))
    for p in range(5):
        sent = mid.at[0, pl.ds(0, W - 1)]
        pltpu.make_async_remote_copy(
            src_ref=sent, dst_ref=sent, send_sem=xs_sem.at[p], recv_sem=xr_sem.at[p],
            device_id=device(x, z, yc), device_id_type=MESH,
        ).wait_send()
        sent = snd.at[0, pl.ds(0, Z - 1)]
        pltpu.make_async_remote_copy(
            src_ref=sent, dst_ref=sent, send_sem=zs_sem.at[p], recv_sem=zr_sem.at[p, 0],
            device_id=device(x, z, yc), device_id_type=MESH,
        ).wait_send()


def finish_kernel(back, out_a, out_b, out_c, out_d):
    choose = choose_matrix()
    for p, pair in enumerate(((out_a, out_b), (out_c, out_d))):
        for b in range(Z):
            turned = lax.dot_general(
                back[p, b].reshape(256, T), choose, (((0,), (0,)), ((), ())), preferred_element_type=F32
            ).astype(BF16)
            for n in range(2):
                pair[n][:, b * 128 : b * 128 + 128] = turned[:, n * 128 : n * 128 + 128]


def local(query_in, key_in, value_in, conv_taps, long_filter, skip_gain, grad_out):
    forward, backward, fine, twist = (jnp.asarray(m) for m in dft_constants())
    anywhere = pl.BlockSpec(memory_space=pl.ANY)
    scalars = pl.BlockSpec(memory_space=pltpu.SMEM)
    vmem = pl.BlockSpec(memory_space=pltpu.VMEM)
    tokens = pltpu.VMEM((T, 1024), BF16)
    back = pl.pallas_call(
        main_kernel,
        out_shape=jax.ShapeDtypeStruct((2, Z, W, 8, T), BF16),
        in_specs=[anywhere] * 5 + [scalars] * 2 + [anywhere] * 4,
        out_specs=vmem,
        scratch_shapes=[
            tokens, tokens, tokens, tokens,
            pltpu.VMEM((T, 1024), F32),
            pltpu.VMEM(forward.shape, BF16),
            pltpu.VMEM(backward.shape, BF16),
            pltpu.VMEM(fine.shape, BF16),
            pltpu.VMEM(twist.shape, F32),
            pltpu.VMEM((256, 256), BF16),
            pltpu.VMEM((3, Z, W, 8, T), BF16),
            pltpu.VMEM((3, W, Z, 8, T), BF16),
            pltpu.VMEM((3, X, Z, 8, 8, T), BF16),
            pltpu.VMEM((2048, T), F32),
            pltpu.VMEM((2, 4, D, 2 * T), F32),
            pltpu.VMEM((2 * D, 2 * T), F32),
            pltpu.VMEM((2, 2 * D, 2 * T), BF16),
            pltpu.VMEM((4, D, T), F32),
            pltpu.VMEM((4, D, T), F32),
            pltpu.VMEM((4, D, T), F32),
            pltpu.VMEM((2, 4, D, T), F32),
            pltpu.VMEM((2, X, Z, 8, 8, T), BF16),
            pltpu.VMEM((2, W, Z, 8, T), BF16),
            pltpu.SemaphoreType.DMA((9,)),
            pltpu.SemaphoreType.DMA((5, X + 1)),
            pltpu.SemaphoreType.DMA((5,)),
            pltpu.SemaphoreType.DMA((5, X)),
            pltpu.SemaphoreType.DMA((5,)),
            pltpu.SemaphoreType.DMA((5,)),
        ],
        compiler_params=pltpu.CompilerParams(
            collective_id=0, has_side_effects=True, vmem_limit_bytes=40 << 20
        ),
        name="hyena_exchange",
    )(query_in, key_in, value_in, grad_out, long_filter, conv_taps, skip_gain, forward, backward, fine, twist)
    result = jax.ShapeDtypeStruct((T, 1024), BF16)
    return tuple(
        pl.pallas_call(
            finish_kernel,
            out_shape=(result,) * 4,
            in_specs=[vmem],
            out_specs=(vmem,) * 4,
            name="hyena_finish",
        )(back)
    )


def solution(mesh):
    tokens = P(("outer", "inner"), None)
    return jax.shard_map(
        local,
        mesh=mesh,
        in_specs=(tokens, tokens, tokens, P(), tokens, P(), tokens),
        out_specs=(tokens,) * 4,
        check_vma=False,
    )
```

profile of v0, /device:TPU:7, one launch (start us, length us, event | category | flops | bytes accessed | tf_op | source)
XLA Modules:
  0.0 106.6 jit_solution(5240866079399783856)
XLA Ops:
  0.6 0.0 copy-start.1
  0.6 1.0 copy-done.1
  1.7 0.0 copy-start.2
  1.7 1.0 copy-done.2
  2.7 0.0 copy-start.3
  2.7 1.0 copy-done.3
  3.8 0.0 copy-start.4
  3.8 1.0 copy-done.4
  4.8 0.0 copy-start.5
  4.8 0.9 copy-done.5
  5.8 0.0 copy-start.6
  5.8 0.9 copy-done.6
  6.7 0.0 copy-start.7
  6.7 0.9 copy-done.7
  7.7 0.0 copy-start.8
  7.7 0.9 copy-done.8
  8.6 0.0 copy-start.9
  8.6 0.9 copy-done.9
  9.6 0.0 copy-start.10
  9.6 0.8 copy-done.10
  10.4 0.0 copy-start.11
  10.4 0.7 copy-done.11
  11.0 92.1 %hyena_exchange.1.back = bf16[2,8,32,8,128]{4,3,2,1,0:T(8,128)(2,1)S(1)} custom-call(bf16[128,1024]{1,0:T(8,128)(2,1)S(1)} %copy-done.5, bf16[128,1024]{1,0:T(8,128)(2,1)S(1)} %copy-done.6, bf16[128,1024]{1,0:T(8,128)(2,1)S(1)} %copy-done.7, bf16[128,1024]{1,0:T(8,128)(2,1)S(1)} %copy-done.8, f32[128,1024]{1,0:T(8,128)S(1)} %copy-done.1, ...), custom_call_target="tpu_custom_call" | custom-call | tf_op jit(solution)/shard_map/hyena_exchange/pallas_call | solution.py:392
  103.1 0.0 copy-start
  103.1 1.0 copy-done
  104.1 2.5 %hyena_finish.1 = (bf16[128,1024]{1,0:T(8,128)(2,1)}, bf16[128,1024]{1,0:T(8,128)(2,1)}, bf16[128,1024]{1,0:T(8,128)(2,1)}, bf16[128,1024]{1,0:T(8,128)(2,1)}) custom-call(bf16[2,8,32,8,128]{4,3,2,1,0:T(8,128)(2,1)} %copy-done), custom_call_target="tpu_custom_call" | custom-call | tf_op jit(solution)/shard_map/hyena_finish/pallas_call | solution.py:432
Async XLA Ops:
  0.6 1.0 copy-start.1
  1.7 1.0 copy-start.2
  2.7 1.0 copy-start.3
  3.8 1.0 copy-start.4
  4.8 0.9 copy-start.5
  5.8 0.9 copy-start.6
  6.7 0.9 copy-start.7
  7.7 0.9 copy-start.8
  8.6 0.9 copy-start.9
  9.6 0.8 copy-start.10
  10.4 0.7 copy-start.11
  103.1 1.0 copy-start
where the time goes:
time: 107 us
  Pallas kernels  94.6 us (88%)
  local copies, waits for them, and re-layouts  11.4 us (11%)
    pallas_call x1, Pallas kernels, local(): pl.pallas_call(main_kernel, out_shape=jax.ShapeDtypeStruct((2, Z, W, 8, T...  92.1 us
    unnamed x24, local copies, waits for them, and re-layouts  11.4 us
    pallas_call x1, Pallas kernels, local(): pl.pallas_call(finish_kernel, out_shape=(result,) * 4, in_specs=[vmem], o...  2.53 us

commit v1 on v0

v1 whole, which is shorter than its diff:
```python
import functools

import jax
import jax.numpy as jnp
import numpy as np
from jax import lax
from jax.experimental import pallas as pl
from jax.experimental.pallas import tpu as pltpu
from jax.sharding import PartitionSpec as P

MESH = pl.DeviceIdType.MESH
F32, BF16 = jnp.float32, jnp.bfloat16
X, Z, Y, C = 4, 8, 4, 2
W = X * Y * C
D = 256
T = 128
POINTS = 2 * D * T


def dft_constants():
    k = np.arange(D)[:, None] + 0.5
    d = np.arange(D)[None, :]
    coarse = 2 * np.pi * (k * d / (2 * D) % 1.0)
    forward = np.concatenate([np.cos(coarse), -np.sin(coarse)], 0)
    backward = np.concatenate([np.cos(coarse).T, -np.sin(coarse).T], 1) * (2.0 / POINTS)
    t = np.arange(T)[None, :]
    turn = 2 * np.pi * (k * t / POINTS % 1.0)
    fine = 2 * np.pi * (t.T * t % T) / T
    c, s = np.cos(fine), np.sin(fine)
    fine_forward = np.block([[c, -s], [s, c]])
    fine_backward = np.block([[c, s], [-s, c]])

    def halves(m):
        m = m.astype(np.float32)
        high = m.astype(jnp.bfloat16)
        low = (m - high.astype(np.float32)).astype(jnp.bfloat16)
        return np.stack([high, low])

    fine_both = np.stack([halves(fine_forward), halves(fine_backward)])
    twist = np.stack([np.cos(turn), np.sin(turn)]).astype(np.float32)
    return halves(forward), halves(backward), fine_both, twist


def place():
    o, i = lax.axis_index("outer"), lax.axis_index("inner")
    return o // 4, (o % 4) * 2 + i // 8, i % 8


def device(x, z, yc):
    return (x * 4 + z // 2, (z % 2) * 8 + yc)


def halves_of(v):
    high = v.astype(BF16)
    return high, (v - high.astype(F32)).astype(BF16)


def dot(a, b):
    return jnp.dot(a, b, preferred_element_type=F32)


def identity():
    r = lax.broadcasted_iota(jnp.int32, (256, 256), 0)
    c = lax.broadcasted_iota(jnp.int32, (256, 256), 1)
    return jnp.where(r == c, 1.0, 0.0).astype(BF16)


K_IN, V_IN, F_HIGH, F_LOW, Q_IN, G_IN, OUT, GRAD_Q, GRAD_K, GRAD_V = range(10)
FINE_PARTS = (G_IN, GRAD_V)
ORDER = (2, 1, 3, 0)


def main_kernel(
    q_hbm, k_hbm, v_hbm, g_hbm, f_hbm, taps, skip, fwd_hbm, bwd_hbm, fine_hbm, twist_hbm,
    back,
    kin, vin, qin, gin, fin, fwd, bwd, fine, twist,
    eye, snd, mid, rcv, rows, spec, coarse, work, gated, mixed, grad, streams, osnd,
    in_sem, local_sem, zs_sem, zr_sem, xs_sem, xr_sem,
):
    x, z, yc = place()
    w = x * 8 + yc

    loads = [
        pltpu.make_async_copy(a, b, in_sem.at[n])
        for n, (a, b) in enumerate(
            [(k_hbm, kin), (v_hbm, vin), (f_hbm, fin), (q_hbm, qin), (g_hbm, gin),
             (fwd_hbm, fwd), (fine_hbm, fine), (twist_hbm, twist), (bwd_hbm, bwd)]
        )
    ]
    for load in loads:
        load.start()

    barrier = pltpu.get_barrier_semaphore()

    def greet_z(i, _):
        pl.semaphore_signal(barrier, inc=1, device_id=device(x, (z + i) % Z, yc), device_id_type=MESH)
        return 0

    def greet_w(i, _):
        there = (w + i) % W
        pl.semaphore_signal(barrier, inc=1, device_id=device(there // 8, z, there % 8), device_id_type=MESH)
        return 0

    lax.fori_loop(1, Z, greet_z, 0)
    lax.fori_loop(1, W, greet_w, 0)
    eye[...] = identity()

    def pack(p, value):
        def block(b, _):
            cols = pl.ds(pl.multiple_of(b * 256, 256), 256)
            turned = lax.dot_general(
                eye[...], value(cols), (((1,), (1,)), ((), ())), preferred_element_type=F32
            )
            snd[p, pl.ds(b * 2, 2)] = turned.reshape(2, W, 4, T).astype(BF16)
            return 0

        lax.fori_loop(0, Z // 2, block, 0)

    def groups_of(p):
        if p in FINE_PARTS:
            return [(n, ((x + dx) % X) * 8, 8) for n, dx in enumerate(ORDER)]
        return [(0, 0, W)]

    def send_z(p, source):
        for n, first, count in groups_of(p):
            def one(dz, _):
                zt = (z + dz) % Z
                pltpu.make_async_remote_copy(
                    src_ref=source(zt, first, count), dst_ref=mid.at[p, pl.ds(first, count), z],
                    send_sem=zs_sem.at[p], recv_sem=zr_sem.at[p, n],
                    device_id=device(x, zt, yc), device_id_type=MESH,
                ).start()
                return 0

            lax.fori_loop(1, Z, one, 0)
            pltpu.make_async_copy(
                source(z, first, count), mid.at[p, pl.ds(first, count), z], local_sem.at[p, n]
            ).start()

    def target_of(p):
        if p < OUT:
            return rcv.at[p, x, :, yc]
        return back.at[p - OUT, :, w]

    def forward(p, group):
        n, first, count = groups_of(p)[group]
        part = mid.at[p, pl.ds(first, count), z]
        pltpu.make_async_copy(part, part, local_sem.at[p, n]).wait()
        arrived = mid.at[p, pl.ds(first, count), pl.ds(0, Z - 1)]
        pltpu.make_async_remote_copy(
            src_ref=arrived, dst_ref=arrived, send_sem=zs_sem.at[p], recv_sem=zr_sem.at[p, n],
            device_id=device(x, z, yc), device_id_type=MESH,
        ).wait_recv()
        target = target_of(p)

        def one_of(dx):
            def one(i, _):
                xt, there = (x + dx) % X, (yc + i) % 8
                pltpu.make_async_remote_copy(
                    src_ref=mid.at[p, xt * 8 + there], dst_ref=target,
                    send_sem=xs_sem.at[p], recv_sem=xr_sem.at[p],
                    device_id=device(xt, z, there), device_id_type=MESH,
                ).start()
                return 0

            return one

        for dx in [ORDER[group]] if p in FINE_PARTS else ORDER:
            lax.fori_loop(1 if dx == 0 else 0, 8, one_of(dx), 0)
            if dx == 0:
                pltpu.make_async_copy(mid.at[p, w], target, local_sem.at[p, X]).start()

    def await_all(p):
        pltpu.make_async_copy(mid.at[p, w], target_of(p), local_sem.at[p, X]).wait()
        part = mid.at[p, pl.ds(0, W - 1)]
        pltpu.make_async_remote_copy(
            src_ref=part, dst_ref=part, send_sem=xs_sem.at[p], recv_sem=xr_sem.at[p],
            device_id=device(x, z, yc), device_id_type=MESH,
        ).wait_recv()

    def unpack(p, slot):
        await_all(p)
        for b in range(X):
            rows[slot, pl.ds(b * 256, 256)] = rcv[p, b].astype(F32).reshape(256, T)

    def row(slot, j):
        return rows[slot, pl.ds(j, D, stride=4), :]

    def put_row(slot, j, value):
        rows[slot, pl.ds(j, D, stride=4), :] = value

    def in_send(p):
        send_z(p, lambda zt, first, count: snd.at[p, zt, pl.ds(first, count)])

    def out_send(p, slot):
        for b in range(X):
            osnd[p - OUT, pl.ds(b * 8, 8)] = (
                rows[slot, pl.ds(b * 256, 256)].reshape(Z, 8, 4, T).swapaxes(0, 1).astype(BF16)
            )
        send_z(p, lambda zt, first, count: osnd.at[p - OUT, pl.ds(first, count), zt])

    def filter_high(cols):
        return fin[:, cols].astype(BF16)

    def filter_low(cols):
        value = fin[:, cols]
        return (value - value.astype(BF16).astype(F32)).astype(BF16)

    loads[0].wait()
    pack(K_IN, lambda cols: kin[:, cols])
    pl.semaphore_wait(barrier, Z + W - 2)
    in_send(K_IN)
    loads[1].wait()
    pack(V_IN, lambda cols: vin[:, cols])
    in_send(V_IN)
    loads[2].wait()
    pack(F_HIGH, filter_high)
    in_send(F_HIGH)
    pack(F_LOW, filter_low)
    in_send(F_LOW)
    loads[3].wait()
    pack(Q_IN, lambda cols: qin[:, cols])
    in_send(Q_IN)
    loads[4].wait()
    pack(G_IN, lambda cols: gin[:, cols])
    in_send(G_IN)
    for load in loads[5:]:
        load.wait()

    lane = lax.broadcasted_iota(jnp.int32, (D, T), 1)
    block_row = lax.broadcasted_iota(jnp.int32, (D, T), 0)

    def delayed(v, n):
        turned = pltpu.roll(v, n, axis=1)
        before = jnp.where(block_row == 0, 0.0, pltpu.roll(turned, 1, axis=0))
        return jnp.where(lane < n, before, turned)

    def advanced(v, n):
        turned = pltpu.roll(v, T - n, axis=1)
        after = jnp.where(block_row == D - 1, 0.0, pltpu.roll(turned, D - 1, axis=0))
        return jnp.where(lane >= T - n, after, turned)

    first_channel = 4 * (z * W + w)

    def short_forward(v, stream, j):
        tap = [taps[stream, n, first_channel + j] for n in range(3)]
        return tap[0] * v + tap[1] * delayed(v, 1) + tap[2] * delayed(v, 2)

    def short_backward(v, stream, j):
        tap = [taps[stream, n, first_channel + j] for n in range(3)]
        return tap[0] * v + tap[1] * advanced(v, 1) + tap[2] * advanced(v, 2)

    def put_columns(v, at):
        high, low = halves_of(v)
        work[0, 0:D, pl.ds(at * T, T)] = high
        work[1, 0:D, pl.ds(at * T, T)] = low

    def transform(out, pair):
        for b in range(2):
            part = pl.ds(b * D, D)
            high = work[0, 0:D]
            coarse[part] = (
                dot(fwd[0, part], high) + dot(fwd[1, part], high) + dot(fwd[0, part], work[1, 0:D])
            )
        tc, ts = twist[0], twist[1]
        for n in range(2):
            cols = pl.ds(n * T, T)
            re, im = coarse[0:D, cols], coarse[D : 2 * D, cols]
            both = jnp.concatenate([re * tc + im * ts, im * tc - re * ts], axis=1)
            high, low = halves_of(both)
            out[2 * pair + n] = (
                dot(high, fine[0, 0]) + dot(low, fine[0, 0]) + dot(high, fine[0, 1])
            )

    def untransform(left, right, conjugate, out, pair):
        tc, ts = twist[0], twist[1]
        for n in range(2):
            a, b = left[2 * pair + n], right[2 * pair + n]
            ar, ai, br, bi = a[:, 0:T], a[:, T:], b[:, 0:T], b[:, T:]
            if conjugate:
                re, im = ar * br + ai * bi, ar * bi - ai * br
            else:
                re, im = ar * br - ai * bi, ar * bi + ai * br
            high, low = halves_of(jnp.concatenate([re, im], axis=1))
            back_spec = dot(high, fine[1, 0]) + dot(low, fine[1, 0]) + dot(high, fine[1, 1])
            gr, gi = back_spec[:, 0:T], back_spec[:, T:]
            cols = pl.ds(n * T, T)
            high, low = halves_of(gr * tc - gi * ts)
            work[0, 0:D, cols] = high
            work[1, 0:D, cols] = low
            high, low = halves_of(gi * tc + gr * ts)
            work[0, D : 2 * D, cols] = high
            work[1, D : 2 * D, cols] = low
        result = dot(bwd[0], work[0]) + dot(bwd[1], work[0]) + dot(bwd[0], work[1])
        for n in range(2):
            out[2 * pair + n] = result[:, n * T : n * T + T]

    def each(count, body):
        def step(i, _):
            body(i)
            return 0

        lax.fori_loop(0, count, step, 0)

    def key_channel(j):
        streams[0, j] = short_forward(row(0, j), 1, j)

    def value_channel(j):
        short_v = short_forward(row(1, j), 2, j)
        streams[1, j] = short_v
        gated[j] = streams[0, j] * short_v

    def gated_pair(pair):
        for n in range(2):
            put_columns(gated[2 * pair + n], n)
        transform(spec.at[1], pair)

    def filter_pair(pair):
        for n in range(2):
            work[0, 0:D, pl.ds(n * T, T)] = row(0, 2 * pair + n).astype(BF16)
            work[1, 0:D, pl.ds(n * T, T)] = row(1, 2 * pair + n).astype(BF16)
        transform(spec.at[0], pair)
        untransform(spec.at[1], spec.at[0], False, mixed, pair)
        for n in range(2):
            j = 2 * pair + n
            mixed[j] = mixed[j] + skip[first_channel + j] * gated[j]

    def query_channel(j):
        short_q = short_forward(row(0, j), 0, j)
        grad[j] = short_q
        put_row(0, j, short_q * mixed[j])

    def upstream_channel(j):
        upstream = row(1, j)
        put_row(1, j, short_backward(upstream * mixed[j], 0, j))
        grad[j] = upstream * grad[j]

    def grad_pair(pair):
        for n in range(2):
            put_columns(grad[2 * pair + n], n)
        transform(spec.at[1], pair)
        untransform(spec.at[0], spec.at[1], True, mixed, pair)
        for n in range(2):
            j = 2 * pair + n
            total = mixed[j] + skip[first_channel + j] * grad[j]
            put_row(0, j, short_backward(total * streams[1, j], 1, j))
            put_row(1, j, short_backward(total * streams[0, j], 2, j))

    forward(K_IN, 0)
    forward(V_IN, 0)
    unpack(K_IN, 0)
    each(4, key_channel)
    unpack(V_IN, 1)
    each(4, value_channel)
    forward(F_HIGH, 0)
    each(2, gated_pair)
    forward(F_LOW, 0)
    unpack(F_HIGH, 0)
    unpack(F_LOW, 1)
    filter_pair(0)
    forward(Q_IN, 0)
    filter_pair(1)
    unpack(Q_IN, 0)
    each(4, query_channel)
    out_send(OUT, 0)
    for group in range(X):
        forward(G_IN, group)
    unpack(G_IN, 1)
    each(4, upstream_channel)
    out_send(GRAD_Q, 1)
    grad_pair(0)
    forward(OUT, 0)
    grad_pair(1)
    out_send(GRAD_K, 0)
    out_send(GRAD_V, 1)
    forward(GRAD_Q, 0)
    forward(GRAD_K, 0)
    for group in range(X):
        forward(GRAD_V, group)
    for p in range(OUT, 10):
        await_all(p)
    for p in range(10):
        sent = mid.at[p, pl.ds(0, W - 1)]
        pltpu.make_async_remote_copy(
            src_ref=sent, dst_ref=sent, send_sem=xs_sem.at[p], recv_sem=xr_sem.at[p],
            device_id=device(x, z, yc), device_id_type=MESH,
        ).wait_send()
        sent = mid.at[p, :, pl.ds(0, Z - 1)]
        pltpu.make_async_remote_copy(
            src_ref=sent, dst_ref=sent, send_sem=zs_sem.at[p], recv_sem=zr_sem.at[p, 0],
            device_id=device(x, z, yc), device_id_type=MESH,
        ).wait_send()


def finish_kernel(back, *outs):
    eye = identity()
    for p in range(4):
        outs[p][...] = lax.dot_general(
            back[p].reshape(256, T), eye, (((0,), (0,)), ((), ())), preferred_element_type=F32
        ).astype(BF16)


def local(query_in, key_in, value_in, conv_taps, long_filter, skip_gain, grad_out):
    forward, backward, fine, twist = (jnp.asarray(m) for m in dft_constants())
    anywhere = pl.BlockSpec(memory_space=pl.ANY)
    scalars = pl.BlockSpec(memory_space=pltpu.SMEM)
    tokens = pltpu.VMEM((T, 1024), BF16)
    back = pl.pallas_call(
        main_kernel,
        out_shape=jax.ShapeDtypeStruct((4, Z, W, 4, T), BF16),
        in_specs=[anywhere] * 5 + [scalars] * 2 + [anywhere] * 4,
        out_specs=pl.BlockSpec(memory_space=pltpu.HBM),
        scratch_shapes=[
            tokens, tokens, tokens, tokens,
            pltpu.VMEM((T, 1024), F32),
            pltpu.VMEM(forward.shape, BF16),
            pltpu.VMEM(backward.shape, BF16),
            pltpu.VMEM(fine.shape, BF16),
            pltpu.VMEM(twist.shape, F32),
            pltpu.VMEM((256, 256), BF16),
            pltpu.VMEM((6, Z, W, 4, T), BF16),
            pltpu.VMEM((10, W, Z, 4, T), BF16),
            pltpu.VMEM((6, X, Z, 8, 4, T), BF16),
            pltpu.VMEM((2, 4 * D, T), F32),
            pltpu.VMEM((2, 4, D, 2 * T), F32),
            pltpu.VMEM((2 * D, 2 * T), F32),
            pltpu.VMEM((2, 2 * D, 2 * T), BF16),
            pltpu.VMEM((4, D, T), F32),
            pltpu.VMEM((4, D, T), F32),
            pltpu.VMEM((4, D, T), F32),
            pltpu.VMEM((2, 4, D, T), F32),
            pltpu.VMEM((4, W, Z, 4, T), BF16),
            pltpu.SemaphoreType.DMA((9,)),
            pltpu.SemaphoreType.DMA((10, X + 1)),
            pltpu.SemaphoreType.DMA((10,)),
            pltpu.SemaphoreType.DMA((10, X)),
            pltpu.SemaphoreType.DMA((10,)),
            pltpu.SemaphoreType.DMA((10,)),
        ],
        compiler_params=pltpu.CompilerParams(
            collective_id=0, has_side_effects=True, vmem_limit_bytes=67043328
        ),
        name="hyena_exchange",
    )(query_in, key_in, value_in, grad_out, long_filter, conv_taps, skip_gain, forward, backward, fine, twist)
    result = jax.ShapeDtypeStruct((T, 1024), BF16)
    return tuple(
        pl.pallas_call(
            finish_kernel,
            out_shape=(result,) * 4,
            grid=(4,),
            in_specs=[pl.BlockSpec((4, 2, W, 4, T), lambda b: (0, b, 0, 0, 0))],
            out_specs=(pl.BlockSpec((T, 256), lambda b: (0, b)),) * 4,
            name="hyena_finish",
        )(back)
    )


def solution(mesh):
    tokens = P(("outer", "inner"), None)
    return jax.shard_map(
        local,
        mesh=mesh,
        in_specs=(tokens, tokens, tokens, P(), tokens, P(), tokens),
        out_specs=(tokens,) * 4,
        check_vma=False,
    )
```

time: 107 us -> 90.7 us (0.85)
  the two profiles are of different devices: /device:TPU:7 before, /device:TPU:1 now
where the time goes in v1:
time: 90.7 us; the launch traced here: 90.5 us
  Pallas kernels  89.8 us (99%)
    pallas_call x1, Pallas kernels, local(): pl.pallas_call(main_kernel, out_shape=jax.ShapeDtypeStruct((4, Z, W, 4, T...  86 us
    pallas_call x1, Pallas kernels, local(): pl.pallas_call(finish_kernel, out_shape=(result,) * 4, grid=(4,), in_spec...  3.8 us

profile of v1, /device:TPU:1, one launch (start us, length us, event | category | flops | bytes accessed | tf_op | source)
XLA Modules:
  0.0 90.5 jit_solution(7973187186560323154)
XLA Ops:
  0.6 86.0 %hyena_exchange.1.back = bf16[4,8,32,4,128]{4,3,2,1,0:T(4,128)(2,1)} custom-call(bf16[128,1024]{1,0:T(8,128)(2,1)} %q_hbm.1, bf16[128,1024]{1,0:T(8,128)(2,1)} %k_hbm.1, bf16[128,1024]{1,0:T(8,128)(2,1)} %v_hbm.1, bf16[128,1024]{1,0:T(8,128)(2,1)} %g_hbm.1, f32[128,1024]{1,0:T(8,128)} %f_hbm.1, f32[3,3,1024]{2,1,0:T(4,128)} %taps.1, f32[1024]{0:T(1024)} %skip.1, ...), custom_call_target="tpu_custom_call" | custom-call | tf_op jit(solution)/shard_map/hyena_exchange/pallas_call | solution.py:408
  86.7 3.8 %hyena_finish.1 = (bf16[128,1024]{1,0:T(8,128)(2,1)}, bf16[128,1024]{1,0:T(8,128)(2,1)}, bf16[128,1024]{1,0:T(8,128)(2,1)}, bf16[128,1024]{1,0:T(8,128)(2,1)}) custom-call(bf16[4,8,32,4,128]{4,3,2,1,0:T(4,128)(2,1)} %hyena_exchange.1.back), custom_call_target="tpu_custom_call" | custom-call | tf_op jit(solution)/shard_map/hyena_finish/pallas_call | solution.py:447

commit v2 on v1

v2 whole, which is shorter than its diff:
```python
import functools

import jax
import jax.numpy as jnp
import numpy as np
from jax import lax
from jax.experimental import pallas as pl
from jax.experimental.pallas import tpu as pltpu
from jax.sharding import PartitionSpec as P

MESH = pl.DeviceIdType.MESH
F32, BF16 = jnp.float32, jnp.bfloat16
X, Z, Y, C = 4, 8, 4, 2
W = X * Y * C
D = 256
T = 128
POINTS = 2 * D * T


def dft_constants():
    k = np.arange(D)[:, None] + 0.5
    d = np.arange(D)[None, :]
    coarse = 2 * np.pi * (k * d / (2 * D) % 1.0)
    forward = np.concatenate([np.cos(coarse), -np.sin(coarse)], 0)
    backward = np.concatenate([np.cos(coarse).T, -np.sin(coarse).T], 1) * (2.0 / POINTS)
    t = np.arange(T)[None, :]
    turn = 2 * np.pi * (k * t / POINTS % 1.0)
    fine = 2 * np.pi * (t.T * t % T) / T
    c, s = np.cos(fine), np.sin(fine)
    fine_forward = np.block([[c, -s], [s, c]])
    fine_backward = np.block([[c, s], [-s, c]])

    def halves(m):
        m = m.astype(np.float32)
        high = m.astype(jnp.bfloat16)
        low = (m - high.astype(np.float32)).astype(jnp.bfloat16)
        return np.stack([high, low])

    fine_both = np.stack([halves(fine_forward), halves(fine_backward)])
    twist = np.stack([np.cos(turn), np.sin(turn)]).astype(np.float32)
    return halves(forward), halves(backward), fine_both, twist


def place():
    o, i = lax.axis_index("outer"), lax.axis_index("inner")
    return o // 4, (o % 4) * 2 + i // 8, i % 8


def device(x, z, yc):
    return (x * 4 + z // 2, (z % 2) * 8 + yc)


def halves_of(v):
    high = v.astype(BF16)
    return high, (v - high.astype(F32)).astype(BF16)


def dot(a, b):
    return jnp.dot(a, b, preferred_element_type=F32)


def identity():
    r = lax.broadcasted_iota(jnp.int32, (256, 256), 0)
    c = lax.broadcasted_iota(jnp.int32, (256, 256), 1)
    return jnp.where(r == c, 1.0, 0.0).astype(BF16)


FILTER, GATED, GRAD_MIXED, CONVOLVED, GRAD_GATED = range(5)
ORDER = (2, 1, 3, 0)
IN_SCALES, CONVOLVED_SCALE, GRAD_SCALE = range(3)

RATIO = 256.0
SHIFT = 124.0 * float(np.log(2.0))
SLOPE = 2.0 * SHIFT / float(np.log(1.0 + RATIO))
FILTER_TOP = 1.125


def encode(v, top):
    size = jnp.exp(SLOPE * jnp.log(1.0 + jnp.abs(v) * (RATIO / top)) - SHIFT)
    return jnp.where(v < 0.0, -size, size)


def decode(code, top):
    size = (jnp.exp((jnp.log(jnp.abs(code)) + SHIFT) * (1.0 / SLOPE)) - 1.0) * (top / RATIO)
    return jnp.where(code < 0.0, -size, size)


def main_kernel(
    q_hbm, k_hbm, v_hbm, g_hbm, f_hbm, taps, skip, fwd_hbm, bwd_hbm, fine_hbm, twist_hbm,
    out_ref, grad_q_ref, grad_k_ref, grad_v_ref,
    kin, vin, qin, gin, fin, fwd, bwd, fine, twist,
    eye, snd, mid, rcv, rows, spec, coarse, work, result, extended, short, gated, grad_mixed, tops,
    osnd, back, before, after, own_scale, mid_scale, in_scale, out_scale, scale_row,
    in_sem, local_sem, zs_sem, zr_sem, xs_sem, xr_sem, halo_s_sem, halo_r_sem,
    scale_local_sem, scale_zs_sem, scale_zr_sem, scale_xs_sem, scale_xr_sem,
):
    x, z, yc = place()
    w = x * 8 + yc
    d = x * 64 + z * 8 + yc
    next_d, last_d = (d + 1) % D, (d + D - 1) % D
    next_device = device(next_d // 64, (next_d // 8) % 8, next_d % 8)
    last_device = device(last_d // 64, (last_d // 8) % 8, last_d % 8)
    here = device(x, z, yc)

    loads = [
        pltpu.make_async_copy(a, b, in_sem.at[n])
        for n, (a, b) in enumerate(
            [(f_hbm, fin), (k_hbm, kin), (v_hbm, vin), (q_hbm, qin), (g_hbm, gin),
             (fwd_hbm, fwd), (fine_hbm, fine), (twist_hbm, twist), (bwd_hbm, bwd)]
        )
    ]
    for load in loads:
        load.start()
    before[...] = jnp.zeros(before.shape, BF16)
    after[...] = jnp.zeros(after.shape, F32)

    barrier = pltpu.get_barrier_semaphore()

    def greet_z(i, _):
        pl.semaphore_signal(barrier, inc=1, device_id=device(x, (z + i) % Z, yc), device_id_type=MESH)
        return 0

    def greet_w(i, _):
        there = (w + i) % W
        pl.semaphore_signal(barrier, inc=1, device_id=device(there // 8, z, there % 8), device_id_type=MESH)
        return 0

    lax.fori_loop(1, Z, greet_z, 0)
    lax.fori_loop(1, W, greet_w, 0)
    for neighbour in (next_device, last_device):
        pl.semaphore_signal(barrier, inc=1, device_id=neighbour, device_id_type=MESH)
    eye[...] = identity()

    def remote(src, dst, send, recv, to):
        return pltpu.make_async_remote_copy(
            src_ref=src, dst_ref=dst, send_sem=send, recv_sem=recv, device_id=to, device_id_type=MESH
        )

    def each(count, body, first=0):
        def step(i, _):
            body(i)
            return 0

        lax.fori_loop(first, count, step, 0)

    def columns_of(b):
        return pl.ds(pl.multiple_of(b * 256, 256), 256)

    def pack(p, code):
        def block(b):
            turned = lax.dot_general(
                eye[...], code(columns_of(b)).astype(BF16), (((1,), (1,)), ((), ())),
                preferred_element_type=F32,
            )
            snd[p, pl.ds(b * 2, 2)] = turned.reshape(2, W, 4, T).astype(BF16)

        each(Z // 2, block)

    def send_z(p, source):
        for n, dx in enumerate(ORDER):
            first = ((x + dx) % X) * 8
            target = mid.at[p, pl.ds(first, 8), z]

            def one(dz):
                zt = (z + dz) % Z
                remote(source(zt, first), target, zs_sem.at[p], zr_sem.at[p, n], device(x, zt, yc)).start()

            each(Z, one, 1)
            pltpu.make_async_copy(source(z, first), target, local_sem.at[p, n]).start()

    def target_of(p):
        if p < CONVOLVED:
            return rcv.at[p, x, :, yc]
        return back.at[p - CONVOLVED, :, w]

    def forward(p, n):
        dx = ORDER[n]
        xt = (x + dx) % X
        part = mid.at[p, pl.ds(xt * 8, 8), z]
        pltpu.make_async_copy(part, part, local_sem.at[p, n]).wait()
        arrived = mid.at[p, pl.ds(xt * 8, 8), pl.ds(0, Z - 1)]
        remote(arrived, arrived, zs_sem.at[p], zr_sem.at[p, n], here).wait_recv()
        target = target_of(p)

        def one(i):
            there = (yc + i) % 8
            remote(mid.at[p, xt * 8 + there], target, xs_sem.at[p], xr_sem.at[p], device(xt, z, there)).start()

        each(8, one, 1 if dx == 0 else 0)
        if dx == 0:
            pltpu.make_async_copy(mid.at[p, w], target, local_sem.at[p, X]).start()

    def await_all(p):
        pltpu.make_async_copy(mid.at[p, w], target_of(p), local_sem.at[p, X]).wait()
        part = mid.at[p, pl.ds(0, W - 1)]
        remote(part, part, xs_sem.at[p], xr_sem.at[p], here).wait_recv()

    def send_scale(n):
        def one(dz):
            remote(
                own_scale.at[n], mid_scale.at[n, z], scale_zs_sem.at[n], scale_zr_sem.at[n],
                device(x, (z + dz) % Z, yc),
            ).start()

        each(Z, one, 1)
        pltpu.make_async_copy(own_scale.at[n], mid_scale.at[n, z], scale_local_sem.at[n, 0]).start()

    def scale_target(n):
        if n == IN_SCALES:
            return in_scale.at[x, :, yc]
        return out_scale.at[n - 1, :, w]

    def forward_scale(n):
        pltpu.make_async_copy(own_scale.at[n], mid_scale.at[n, z], scale_local_sem.at[n, 0]).wait()
        arrived = mid_scale.at[n, pl.ds(0, Z - 1)]
        remote(arrived, arrived, scale_zs_sem.at[n], scale_zr_sem.at[n], here).wait_recv()

        def one(i):
            there = (w + i) % W
            remote(
                mid_scale.at[n], scale_target(n), scale_xs_sem.at[n], scale_xr_sem.at[n],
                device(there // 8, z, there % 8),
            ).start()

        each(W, one, 1)
        pltpu.make_async_copy(mid_scale.at[n], scale_target(n), scale_local_sem.at[n, 1]).start()

    def await_scale(n):
        pltpu.make_async_copy(mid_scale.at[n], scale_target(n), scale_local_sem.at[n, 1]).wait()
        part = out_scale.at[0, :, pl.ds(0, W - 1)]
        remote(part, part, scale_xs_sem.at[n], scale_xr_sem.at[n], here).wait_recv()

    def in_send(p):
        send_z(p, lambda zt, first: snd.at[p, zt, pl.ds(first, 8)])

    loads[0].wait()
    pack(FILTER, lambda cols: encode(fin[:, cols], FILTER_TOP))
    for load in loads[1:5]:
        load.wait()
    pl.semaphore_wait(barrier, Z + W)
    streams = (qin, kin, vin)
    halos = [
        remote(stream.at[pl.ds(T - 16, 16)], before.at[n], halo_s_sem.at[n], halo_r_sem.at[n], next_device)
        for n, stream in enumerate(streams)
    ]

    @pl.when(d != D - 1)
    def _():
        for halo in halos:
            halo.start()

    in_send(FILTER)

    @pl.when(d != 0)
    def _():
        for halo in halos:
            halo.wait_recv()

    tops[...] = jnp.zeros(tops.shape, F32)

    def gate_block(b):
        cols = columns_of(b)
        for n, stream in enumerate(streams):
            extended[n, 0:8, cols] = before[n, :, cols].astype(F32)[8:16]
            extended[n, 8 : T + 8, cols] = stream[:, cols].astype(F32)
            short[n, :, cols] = (
                taps[n, 0:1, cols] * extended[n, 8 : T + 8, cols]
                + taps[n, 1:2, cols] * extended[n, 7 : T + 7, cols]
                + taps[n, 2:3, cols] * extended[n, 6 : T + 6, cols]
            )
        value = short[1, :, cols] * short[2, :, cols]
        gated[:, cols] = value
        tops[0] = jnp.maximum(tops[0], jnp.max(jnp.abs(value).reshape(16, 8, 256), axis=0))
        value = gin[:, cols].astype(F32) * short[0, :, cols]
        grad_mixed[:, cols] = value
        tops[1] = jnp.maximum(tops[1], jnp.max(jnp.abs(value).reshape(16, 8, 256), axis=0))

    each(4, gate_block)

    def top_of(n):
        return jnp.maximum(jnp.max(tops[n], keepdims=True), 1e-30)

    gated_top, grad_top = top_of(0), top_of(1)
    first_half = lax.broadcasted_iota(jnp.int32, (1, T), 1) < T // 2
    own_scale[IN_SCALES] = jnp.where(first_half, gated_top, grad_top)
    pack(GATED, lambda cols: encode(gated[:, cols], gated_top))
    send_scale(IN_SCALES)
    in_send(GATED)
    pack(GRAD_MIXED, lambda cols: encode(grad_mixed[:, cols], grad_top))
    in_send(GRAD_MIXED)
    for load in loads[5:]:
        load.wait()

    def unpack(p):
        await_all(p)
        for b in range(X):
            rows[pl.ds(b * 256, 256)] = rcv[p, b].astype(F32).reshape(256, T)

    def row(j):
        return rows[pl.ds(j, D, stride=4), :]

    def put_columns(v, at):
        high, low = halves_of(v)
        work[0, 0:D, pl.ds(at * T, T)] = high
        work[1, 0:D, pl.ds(at * T, T)] = low

    def transform(out, pair):
        for b in range(2):
            part = pl.ds(b * D, D)
            high = work[0, 0:D]
            coarse[part] = (
                dot(fwd[0, part], high) + dot(fwd[1, part], high) + dot(fwd[0, part], work[1, 0:D])
            )
        tc, ts = twist[0], twist[1]
        for n in range(2):
            cols = pl.ds(n * T, T)
            re, im = coarse[0:D, cols], coarse[D : 2 * D, cols]
            both = jnp.concatenate([re * tc + im * ts, im * tc - re * ts], axis=1)
            high, low = halves_of(both)
            out[2 * pair + n] = (
                dot(high, fine[0, 0]) + dot(low, fine[0, 0]) + dot(high, fine[0, 1])
            )

    def untransform(left, right, conjugate, out, pair):
        tc, ts = twist[0], twist[1]
        for n in range(2):
            a, b = left[2 * pair + n], right[2 * pair + n]
            ar, ai, br, bi = a[:, 0:T], a[:, T:], b[:, 0:T], b[:, T:]
            if conjugate:
                re, im = ar * br + ai * bi, ar * bi - ai * br
            else:
                re, im = ar * br - ai * bi, ar * bi + ai * br
            high, low = halves_of(jnp.concatenate([re, im], axis=1))
            back_spec = dot(high, fine[1, 0]) + dot(low, fine[1, 0]) + dot(high, fine[1, 1])
            gr, gi = back_spec[:, 0:T], back_spec[:, T:]
            cols = pl.ds(n * T, T)
            high, low = halves_of(gr * tc - gi * ts)
            work[0, 0:D, cols] = high
            work[1, 0:D, cols] = low
            high, low = halves_of(gi * tc + gr * ts)
            work[0, D : 2 * D, cols] = high
            work[1, D : 2 * D, cols] = low
        value = dot(bwd[0], work[0]) + dot(bwd[1], work[0]) + dot(bwd[0], work[1])
        for n in range(2):
            out[2 * pair + n] = value[:, n * T : n * T + T]

    def filter_pair(pair):
        for n in range(2):
            put_columns(decode(row(2 * pair + n), FILTER_TOP), n)
        transform(spec.at[0], pair)

    def convolve_pair(half, conjugate):
        def body(pair):
            top = jnp.broadcast_to(
                in_scale[...].reshape(D, T)[:, half * 64 : half * 64 + 1], (D, T)
            )
            for n in range(2):
                put_columns(decode(row(2 * pair + n), top), n)
            transform(spec.at[1], pair)
            untransform(spec.at[0], spec.at[1], conjugate, result, pair)

        return body

    def out_send(p):
        top = jnp.max(jnp.max(jnp.abs(result[...]), axis=0), keepdims=True)
        top = jnp.maximum(top, 1e-30)
        own_scale[p - CONVOLVED + 1] = jnp.broadcast_to(top, (1, T))

        def code_row(j):
            rows[pl.ds(j, D, stride=4), :] = encode(result[j], top)

        each(4, code_row)
        for b in range(X):
            osnd[p - CONVOLVED, pl.ds(b * 8, 8)] = (
                rows[pl.ds(b * 256, 256)].reshape(Z, 8, 4, T).swapaxes(0, 1).astype(BF16)
            )
        send_scale(p - CONVOLVED + 1)
        send_z(p, lambda zt, first: osnd.at[p - CONVOLVED, pl.ds(first, 8), zt])

    for n in range(X):
        forward(FILTER, n)
    forward_scale(IN_SCALES)
    unpack(FILTER)
    each(2, filter_pair)
    for n in range(X):
        forward(GATED, n)
    await_scale(IN_SCALES)
    unpack(GATED)
    conv = convolve_pair(0, False)
    conv(0)
    for n in range(X):
        forward(GRAD_MIXED, n)
    conv(1)
    out_send(CONVOLVED)
    unpack(GRAD_MIXED)
    each(2, convolve_pair(1, True))
    out_send(GRAD_GATED)
    forward_scale(CONVOLVED_SCALE)
    for n in range(X):
        forward(CONVOLVED, n)
    forward_scale(GRAD_SCALE)

    def make_scale_row(n):
        await_scale(n + 1)
        owner = lax.broadcasted_iota(jnp.int32, (D, 1024), 0)
        channel = lax.broadcasted_iota(jnp.int32, (D, 1024), 1)
        top = jnp.tile(out_scale[n].reshape(D, T), (1, 8))
        scale_row[n : n + 1] = jnp.sum(jnp.where(channel // 4 == owner, top, 0.0), axis=0, keepdims=True)

    def returned(n, b):
        cols = columns_of(b)
        code = lax.dot_general(
            back[n, pl.ds(b * 2, 2)].reshape(256, T), eye[...], (((0,), (0,)), ((), ())),
            preferred_element_type=F32,
        )
        return decode(code, scale_row[n : n + 1, cols])

    def backward_halo(n):
        return remote(
            extended.at[n, pl.ds(0, 8)], after.at[n], halo_s_sem.at[3 + n], halo_r_sem.at[3 + n], last_device
        )

    def send_halo(n):
        @pl.when(d != 0)
        def _():
            backward_halo(n).start()

    def await_halo(n):
        @pl.when(d != D - 1)
        def _():
            backward_halo(n).wait_recv()

    def mix_block(b):
        cols = columns_of(b)
        mixed = returned(0, b) + skip[:, cols] * gated[:, cols]
        out_ref[:, cols] = (short[0, :, cols] * mixed).astype(BF16)
        extended[0, 0:T, cols] = gin[:, cols].astype(F32) * mixed

    def grad_block(b):
        cols = columns_of(b)
        total = returned(1, b) + skip[:, cols] * grad_mixed[:, cols]
        extended[1, 0:T, cols] = total * short[2, :, cols]
        extended[2, 0:T, cols] = total * short[1, :, cols]

    def finish(n, ref):
        def block(b):
            cols = columns_of(b)
            extended[n, T : T + 8, cols] = after[n, :, cols]
            ref[:, cols] = (
                taps[n, 0:1, cols] * extended[n, 0:T, cols]
                + taps[n, 1:2, cols] * extended[n, 1 : T + 1, cols]
                + taps[n, 2:3, cols] * extended[n, 2 : T + 2, cols]
            ).astype(BF16)

        each(4, block)

    make_scale_row(0)
    await_all(CONVOLVED)
    each(4, mix_block)
    send_halo(0)
    for n in range(X):
        forward(GRAD_GATED, n)
    make_scale_row(1)
    await_all(GRAD_GATED)
    each(4, grad_block)
    send_halo(1)
    send_halo(2)
    await_halo(0)
    finish(0, grad_q_ref)
    await_halo(1)
    finish(1, grad_k_ref)
    await_halo(2)
    finish(2, grad_v_ref)

    @pl.when(d != D - 1)
    def _():
        for halo in halos:
            halo.wait_send()

    @pl.when(d != 0)
    def _():
        for n in range(3):
            backward_halo(n).wait_send()

    for p in range(5):
        sent = mid.at[p, pl.ds(0, W - 1)]
        remote(sent, sent, xs_sem.at[p], xr_sem.at[p], here).wait_send()
        sent = mid.at[p, :, pl.ds(0, Z - 1)]
        remote(sent, sent, zs_sem.at[p], zr_sem.at[p, 0], here).wait_send()
    for n in range(3):
        sent = out_scale.at[0, :, pl.ds(0, W - 1)]
        remote(sent, sent, scale_xs_sem.at[n], scale_xr_sem.at[n], here).wait_send()
        sent = mid_scale.at[n, pl.ds(0, Z - 1)]
        remote(sent, sent, scale_zs_sem.at[n], scale_zr_sem.at[n], here).wait_send()


def local(query_in, key_in, value_in, conv_taps, long_filter, skip_gain, grad_out):
    forward, backward, fine, twist = (jnp.asarray(m) for m in dft_constants())
    anywhere = pl.BlockSpec(memory_space=pltpu.HBM)
    vmem = pl.BlockSpec(memory_space=pltpu.VMEM)
    tokens = pltpu.VMEM((T, 1024), BF16)
    wide = pltpu.VMEM((T, 1024), F32)
    result = jax.ShapeDtypeStruct((T, 1024), BF16)
    dma = pltpu.SemaphoreType.DMA
    return tuple(
        pl.pallas_call(
            main_kernel,
            out_shape=(result,) * 4,
            in_specs=[anywhere] * 5 + [vmem] * 2 + [anywhere] * 4,
            out_specs=(vmem,) * 4,
            scratch_shapes=[
                tokens, tokens, tokens, tokens, wide,
                pltpu.VMEM(forward.shape, BF16),
                pltpu.VMEM(backward.shape, BF16),
                pltpu.VMEM(fine.shape, BF16),
                pltpu.VMEM(twist.shape, F32),
                pltpu.VMEM((256, 256), BF16),
                pltpu.VMEM((3, Z, W, 4, T), BF16),
                pltpu.VMEM((5, W, Z, 4, T), BF16),
                pltpu.VMEM((3, X, Z, 8, 4, T), BF16),
                pltpu.VMEM((4 * D, T), F32),
                pltpu.VMEM((2, 4, D, 2 * T), F32),
                pltpu.VMEM((2 * D, 2 * T), F32),
                pltpu.VMEM((2, 2 * D, 2 * T), BF16),
                pltpu.VMEM((4, D, T), F32),
                pltpu.VMEM((3, T + 8, 1024), F32),
                pltpu.VMEM((3, T, 1024), F32),
                wide, wide,
                pltpu.VMEM((2, 8, 256), F32),
                pltpu.VMEM((2, W, Z, 4, T), BF16),
                pltpu.VMEM((2, Z, W, 4, T), BF16),
                pltpu.VMEM((3, 16, 1024), BF16),
                pltpu.VMEM((3, 8, 1024), F32),
                pltpu.VMEM((3, 1, T), F32),
                pltpu.VMEM((3, Z, 1, T), F32),
                pltpu.VMEM((X, Z, 8, 1, T), F32),
                pltpu.VMEM((2, Z, W, 1, T), F32),
                pltpu.VMEM((2, 1024), F32),
                dma((9,)), dma((5, X + 1)), dma((5,)), dma((5, X)), dma((5,)), dma((5,)),
                dma((6,)), dma((6,)),
                dma((3, 2)), dma((3,)), dma((3,)), dma((3,)), dma((3,)),
            ],
            compiler_params=pltpu.CompilerParams(
                collective_id=0, has_side_effects=True, vmem_limit_bytes=67043328
            ),
            name="hyena_exchange",
        )(
            query_in, key_in, value_in, grad_out, long_filter, conv_taps, skip_gain.reshape(1, 1024),
            forward, backward, fine, twist,
        )
    )


def solution(mesh):
    tokens = P(("outer", "inner"), None)
    return jax.shard_map(
        local,
        mesh=mesh,
        in_specs=(tokens, tokens, tokens, P(), tokens, P(), tokens),
        out_specs=(tokens,) * 4,
        check_vma=False,
    )
```

time: 90.7 us -> 76.4 us (0.84)
  Pallas kernels: 89.8 us -> 71.1 us
  local copies, waits for them, and re-layouts: 0 us -> 4.5 us
    pallas_call x2 -> x1, Pallas kernels: 89.8 us -> 71.1 us  [local(): pl.pallas_call(main_kernel, out_shape=(result,) * 4, in_specs=[anywhere]...]
    unnamed x0 -> x10, local copies, waits for them, and re-layouts: none -> 4.5 us
where the time goes in v2:
time: 76.4 us; the launch traced here: 76.2 us
  Pallas kernels  71.1 us (93%)
  local copies, waits for them, and re-layouts  4.5 us (6%)
    pallas_call x1, Pallas kernels, local(): pl.pallas_call(main_kernel, out_shape=(result,) * 4, in_specs=[anywhere]...  71.1 us
    unnamed x10, local copies, waits for them, and re-layouts  4.5 us

profile of v2, /device:TPU:1, one launch (start us, length us, event | category | flops | bytes accessed | tf_op | source)
XLA Modules:
  0.0 76.2 jit_solution(15268561426218936028)
XLA Ops:
  0.6 71.1 %hyena_exchange.1 = (bf16[128,1024]{1,0:T(8,128)(2,1)}, bf16[128,1024]{1,0:T(8,128)(2,1)}, bf16[128,1024]{1,0:T(8,128)(2,1)}, bf16[128,1024]{1,0:T(8,128)(2,1)}) custom-call(bf16[128,1024]{1,0:T(8,128)(2,1)} %q_hbm.1, bf16[128,1024]{1,0:T(8,128)(2,1)} %k_hbm.1, bf16[128,1024]{1,0:T(8,128)(2,1)} %v_hbm.1, bf16[128,1024]{1,0:T(8,128)(2,1)} %g_hbm.1, ...), custom_call_target="tpu_custom_call" | custom-call | tf_op jit(solution)/shard_map/hyena_exchange/pallas_call | solution.py:506
  71.7 0.0 copy-start.2
  71.7 1.7 %copy.19 = bf16[128,1024]{1,0:T(8,128)(2,1)} copy(bf16[128,1024]{1,0:T(8,128)(2,1)} %get-tuple-element.8) | data formatting | bytes 524288
  73.4 0.0 copy-done.2
  73.4 0.0 copy-start.1
  73.4 0.7 copy.20
  74.1 0.3 copy-done.1
  74.5 0.0 copy-start
  74.5 0.7 copy.21
  75.2 0.3 copy-done
  75.5 0.7 copy.22
Async XLA Ops:
  71.7 1.7 %copy-start.2 = (bf16[128,1024]{1,0:T(8,128)(2,1)S(1)}, bf16[128,1024]{1,0:T(8,128)(2,1)}, u32[]{:S(2)}) copy-start(bf16[128,1024]{1,0:T(8,128)(2,1)} %get-tuple-element.9) | copy-start | bytes 786436
  73.4 1.0 %copy-start.1 = (bf16[128,1024]{1,0:T(8,128)(2,1)S(1)}, bf16[128,1024]{1,0:T(8,128)(2,1)}, u32[]{:S(2)}) copy-start(bf16[128,1024]{1,0:T(8,128)(2,1)} %get-tuple-element.10) | copy-start | bytes 786436
  74.5 1.0 %copy-start = (bf16[128,1024]{1,0:T(8,128)(2,1)S(1)}, bf16[128,1024]{1,0:T(8,128)(2,1)}, u32[]{:S(2)}) copy-start(bf16[128,1024]{1,0:T(8,128)(2,1)} %get-tuple-element.11) | copy-start | bytes 786436

commit v3 on v2

--- a/solution.py
+++ b/solution.py
@@ -143,6 +143,10 @@
 
         lax.fori_loop(first, count, step, 0)
 
+    def all_of(count, body, first=0):
+        for i in range(first, count):
+            body(i)
+
     def columns_of(b):
         return pl.ds(pl.multiple_of(b * 256, 256), 256)
 
@@ -165,7 +169,7 @@
                 zt = (z + dz) % Z
                 remote(source(zt, first), target, zs_sem.at[p], zr_sem.at[p, n], device(x, zt, yc)).start()
 
-            each(Z, one, 1)
+            all_of(Z, one, 1)
             pltpu.make_async_copy(source(z, first), target, local_sem.at[p, n]).start()
 
     def target_of(p):
@@ -186,7 +190,7 @@
             there = (yc + i) % 8
             remote(mid.at[p, xt * 8 + there], target, xs_sem.at[p], xr_sem.at[p], device(xt, z, there)).start()
 
-        each(8, one, 1 if dx == 0 else 0)
+        all_of(8, one, 1 if dx == 0 else 0)
         if dx == 0:
             pltpu.make_async_copy(mid.at[p, w], target, local_sem.at[p, X]).start()
 
@@ -202,7 +206,7 @@
                 device(x, (z + dz) % Z, yc),
             ).start()
 
-        each(Z, one, 1)
+        all_of(Z, one, 1)
         pltpu.make_async_copy(own_scale.at[n], mid_scale.at[n, z], scale_local_sem.at[n, 0]).start()
 
     def scale_target(n):
@@ -222,7 +226,7 @@
                 device(there // 8, z, there % 8),
             ).start()
 
-        each(W, one, 1)
+        all_of(W, one, 1)
         pltpu.make_async_copy(mid_scale.at[n], scale_target(n), scale_local_sem.at[n, 1]).start()
 
     def await_scale(n):
@@ -494,6 +498,19 @@
         remote(sent, sent, scale_zs_sem.at[n], scale_zr_sem.at[n], here).wait_send()
 
 
+def hand_on_kernel(*refs):
+    ins, outs, (held, in_sem, out_sem) = refs[:4], refs[4:8], refs[8:]
+    inward = [pltpu.make_async_copy(ins[n], held.at[n], in_sem.at[n]) for n in range(4)]
+    outward = [pltpu.make_async_copy(held.at[n], outs[n], out_sem.at[n]) for n in range(4)]
+    for copy in inward:
+        copy.start()
+    for n in range(4):
+        inward[n].wait()
+        outward[n].start()
+    for copy in outward:
+        copy.wait()
+
+
 def local(query_in, key_in, value_in, conv_taps, long_filter, skip_gain, grad_out):
     forward, backward, fine, twist = (jnp.asarray(m) for m in dft_constants())
     anywhere = pl.BlockSpec(memory_space=pltpu.HBM)
@@ -502,52 +519,62 @@
     wide = pltpu.VMEM((T, 1024), F32)
     result = jax.ShapeDtypeStruct((T, 1024), BF16)
     dma = pltpu.SemaphoreType.DMA
+    outs = pl.pallas_call(
+        main_kernel,
+        out_shape=(result,) * 4,
+        in_specs=[anywhere] * 5 + [vmem] * 2 + [anywhere] * 4,
+        out_specs=(vmem,) * 4,
+        scratch_shapes=[
+            tokens, tokens, tokens, tokens, wide,
+            pltpu.VMEM(forward.shape, BF16),
+            pltpu.VMEM(backward.shape, BF16),
+            pltpu.VMEM(fine.shape, BF16),
+            pltpu.VMEM(twist.shape, F32),
+            pltpu.VMEM((256, 256), BF16),
+            pltpu.VMEM((3, Z, W, 4, T), BF16),
+            pltpu.VMEM((5, W, Z, 4, T), BF16),
+            pltpu.VMEM((3, X, Z, 8, 4, T), BF16),
+            pltpu.VMEM((4 * D, T), F32),
+            pltpu.VMEM((2, 4, D, 2 * T), F32),
+            pltpu.VMEM((2 * D, 2 * T), F32),
+            pltpu.VMEM((2, 2 * D, 2 * T), BF16),
+            pltpu.VMEM((4, D, T), F32),
+            pltpu.VMEM((3, T + 8, 1024), F32),
+            pltpu.VMEM((3, T, 1024), F32),
+            wide, wide,
+            pltpu.VMEM((2, 8, 256), F32),
+            pltpu.VMEM((2, W, Z, 4, T), BF16),
+            pltpu.VMEM((2, Z, W, 4, T), BF16),
+            pltpu.VMEM((3, 16, 1024), BF16),
+            pltpu.VMEM((3, 8, 1024), F32),
+            pltpu.VMEM((3, 1, T), F32),
+            pltpu.VMEM((3, Z, 1, T), F32),
+            pltpu.VMEM((X, Z, 8, 1, T), F32),
+            pltpu.VMEM((2, Z, W, 1, T), F32),
+            pltpu.VMEM((2, 1024), F32),
+            dma((9,)), dma((5, X + 1)), dma((5,)), dma((5, X)), dma((5,)), dma((5,)),
+            dma((6,)), dma((6,)),
+            dma((3, 2)), dma((3,)), dma((3,)), dma((3,)), dma((3,)),
+        ],
+        compiler_params=pltpu.CompilerParams(
+            collective_id=0, has_side_effects=True, vmem_limit_bytes=67043328
+        ),
+        name="hyena_exchange",
+    )(
+        query_in, key_in, value_in, grad_out, long_filter, conv_taps, skip_gain.reshape(1, 1024),
+        forward, backward, fine, twist,
+    )
+    anyhow = pl.BlockSpec(memory_space=pltpu.HBM)
     return tuple(
         pl.pallas_call(
-            main_kernel,
+            hand_on_kernel,
             out_shape=(result,) * 4,
-            in_specs=[anywhere] * 5 + [vmem] * 2 + [anywhere] * 4,
-            out_specs=(vmem,) * 4,
-            scratch_shapes=[
-                tokens, tokens, tokens, tokens, wide,
-                pltpu.VMEM(forward.shape, BF16),
-                pltpu.VMEM(backward.shape, BF16),
-                pltpu.VMEM(fine.shape, BF16),
-                pltpu.VMEM(twist.shape, F32),
-                pltpu.VMEM((256, 256), BF16),
-                pltpu.VMEM((3, Z, W, 4, T), BF16),
-                pltpu.VMEM((5, W, Z, 4, T), BF16),
-                pltpu.VMEM((3, X, Z, 8, 4, T), BF16),
-                pltpu.VMEM((4 * D, T), F32),
-                pltpu.VMEM((2, 4, D, 2 * T), F32),
-                pltpu.VMEM((2 * D, 2 * T), F32),
-                pltpu.VMEM((2, 2 * D, 2 * T), BF16),
-                pltpu.VMEM((4, D, T), F32),
-                pltpu.VMEM((3, T + 8, 1024), F32),
-                pltpu.VMEM((3, T, 1024), F32),
-                wide, wide,
-                pltpu.VMEM((2, 8, 256), F32),
-                pltpu.VMEM((2, W, Z, 4, T), BF16),
-                pltpu.VMEM((2, Z, W, 4, T), BF16),
-                pltpu.VMEM((3, 16, 1024), BF16),
-                pltpu.VMEM((3, 8, 1024), F32),
-                pltpu.VMEM((3, 1, T), F32),
-                pltpu.VMEM((3, Z, 1, T), F32),
-                pltpu.VMEM((X, Z, 8, 1, T), F32),
-                pltpu.VMEM((2, Z, W, 1, T), F32),
-                pltpu.VMEM((2, 1024), F32),
-                dma((9,)), dma((5, X + 1)), dma((5,)), dma((5, X)), dma((5,)), dma((5,)),
-                dma((6,)), dma((6,)),
-                dma((3, 2)), dma((3,)), dma((3,)), dma((3,)), dma((3,)),
-            ],
-            compiler_params=pltpu.CompilerParams(
-                collective_id=0, has_side_effects=True, vmem_limit_bytes=67043328
-            ),
-            name="hyena_exchange",
-        )(
-            query_in, key_in, value_in, grad_out, long_filter, conv_taps, skip_gain.reshape(1, 1024),
-            forward, backward, fine, twist,
-        )
+            in_specs=[anyhow] * 4,
+            out_specs=(anyhow,) * 4,
+            scratch_shapes=[pltpu.VMEM((4, T, 1024), BF16), dma((4,)), dma((4,))],
+            compiler_params=pltpu.CompilerParams(vmem_limit_bytes=67043328),
+            name="hyena_hand_on",
+        )(*outs)
     )
 
 

time: 76.4 us -> 72.2 us (0.945)
  local copies, waits for them, and re-layouts: 4.5 us -> 0 us
    unnamed x10 -> x0, local copies, waits for them, and re-layouts: 4.5 us -> none
    pallas_call x0 -> x1, Pallas kernels: none -> 1.98 us  [local(): pl.pallas_call(hand_on_kernel, out_shape=(result,) * 4, in_specs=[anyhow]...]
    pallas_call x1, Pallas kernels: 71.1 us -> 69.5 us  [local(): pl.pallas_call(main_kernel, out_shape=(result,) * 4, in_specs=[anywhere]...]
where the time goes in v3:
time: 72.2 us; the launch traced here: 72.1 us
  Pallas kernels  71.4 us (99%)
    pallas_call x1, Pallas kernels, local(): pl.pallas_call(main_kernel, out_shape=(result,) * 4, in_specs=[anywhere]...  69.5 us
    pallas_call x1, Pallas kernels, local(): pl.pallas_call(hand_on_kernel, out_shape=(result,) * 4, in_specs=[anyhow]...  1.98 us

profile of v3, /device:TPU:1, one launch (start us, length us, event | category | flops | bytes accessed | tf_op | source)
XLA Modules:
  0.0 72.1 jit_solution(16696154706687709167)
XLA Ops:
  0.6 69.5 %hyena_exchange.1 = (bf16[128,1024]{1,0:T(8,128)(2,1)}, bf16[128,1024]{1,0:T(8,128)(2,1)}, bf16[128,1024]{1,0:T(8,128)(2,1)}, bf16[128,1024]{1,0:T(8,128)(2,1)}) custom-call(bf16[128,1024]{1,0:T(8,128)(2,1)} %q_hbm.1, bf16[128,1024]{1,0:T(8,128)(2,1)} %k_hbm.1, bf16[128,1024]{1,0:T(8,128)(2,1)} %v_hbm.1, bf16[128,1024]{1,0:T(8,128)(2,1)} %g_hbm.1, ...), custom_call_target="tpu_custom_call" | custom-call | tf_op jit(solution)/shard_map/hyena_exchange/pallas_call | solution.py:522
  70.1 2.0 %hyena_hand_on.1 = (bf16[128,1024]{1,0:T(8,128)(2,1)}, bf16[128,1024]{1,0:T(8,128)(2,1)}, bf16[128,1024]{1,0:T(8,128)(2,1)}, bf16[128,1024]{1,0:T(8,128)(2,1)}) custom-call(bf16[128,1024]{1,0:T(8,128)(2,1)} %get-tuple-element.8.refs_0_, bf16[128,1024]{1,0:T(8,128)(2,1)} %get-tuple-element.9.refs_1_, bf16[128,1024]{1,0:T(8,128)(2,1)} %get-tuple-element.10.refs_2_, ...), custom_call_target="tpu_custom_call" | custom-call | tf_op jit(solution)/shard_map/hyena_hand_on/pallas_call | solution.py:569

commit v4 on v3

--- a/solution.py
+++ b/solution.py
@@ -87,11 +87,11 @@
 
 def main_kernel(
     q_hbm, k_hbm, v_hbm, g_hbm, f_hbm, taps, skip, fwd_hbm, bwd_hbm, fine_hbm, twist_hbm,
-    out_ref, grad_q_ref, grad_k_ref, grad_v_ref,
+    out_hbm, grad_q_hbm, grad_k_hbm, grad_v_hbm,
     kin, vin, qin, gin, fin, fwd, bwd, fine, twist,
     eye, snd, mid, rcv, rows, spec, coarse, work, result, extended, short, gated, grad_mixed, tops,
-    osnd, back, before, after, own_scale, mid_scale, in_scale, out_scale, scale_row,
-    in_sem, local_sem, zs_sem, zr_sem, xs_sem, xr_sem, halo_s_sem, halo_r_sem,
+    osnd, back, before, after, own_scale, mid_scale, in_scale, out_scale, scale_row, held,
+    in_sem, held_sem, local_sem, zs_sem, zr_sem, xs_sem, xr_sem, halo_s_sem, halo_r_sem,
     scale_local_sem, scale_zs_sem, scale_zr_sem, scale_xs_sem, scale_xr_sem,
 ):
     x, z, yc = place()
@@ -437,7 +437,7 @@
     def mix_block(b):
         cols = columns_of(b)
         mixed = returned(0, b) + skip[:, cols] * gated[:, cols]
-        out_ref[:, cols] = (short[0, :, cols] * mixed).astype(BF16)
+        held[0, :, cols] = (short[0, :, cols] * mixed).astype(BF16)
         extended[0, 0:T, cols] = gin[:, cols].astype(F32) * mixed
 
     def grad_block(b):
@@ -446,22 +446,29 @@
         extended[1, 0:T, cols] = total * short[2, :, cols]
         extended[2, 0:T, cols] = total * short[1, :, cols]
 
-    def finish(n, ref):
+    results = [
+        pltpu.make_async_copy(held.at[n], ref, held_sem.at[n])
+        for n, ref in enumerate((out_hbm, grad_q_hbm, grad_k_hbm, grad_v_hbm))
+    ]
+
+    def finish(n):
         def block(b):
             cols = columns_of(b)
             extended[n, T : T + 8, cols] = after[n, :, cols]
-            ref[:, cols] = (
+            held[n + 1, :, cols] = (
                 taps[n, 0:1, cols] * extended[n, 0:T, cols]
                 + taps[n, 1:2, cols] * extended[n, 1 : T + 1, cols]
                 + taps[n, 2:3, cols] * extended[n, 2 : T + 2, cols]
             ).astype(BF16)
 
         each(4, block)
+        results[n + 1].start()
 
     make_scale_row(0)
     await_all(CONVOLVED)
     each(4, mix_block)
     send_halo(0)
+    results[0].start()
     for n in range(X):
         forward(GRAD_GATED, n)
     make_scale_row(1)
@@ -470,11 +477,11 @@
     send_halo(1)
     send_halo(2)
     await_halo(0)
-    finish(0, grad_q_ref)
+    finish(0)
     await_halo(1)
-    finish(1, grad_k_ref)
+    finish(1)
     await_halo(2)
-    finish(2, grad_v_ref)
+    finish(2)
 
     @pl.when(d != D - 1)
     def _():
@@ -486,6 +493,8 @@
         for n in range(3):
             backward_halo(n).wait_send()
 
+    for copy in results:
+        copy.wait()
     for p in range(5):
         sent = mid.at[p, pl.ds(0, W - 1)]
         remote(sent, sent, xs_sem.at[p], xr_sem.at[p], here).wait_send()
@@ -523,7 +532,7 @@
         main_kernel,
         out_shape=(result,) * 4,
         in_specs=[anywhere] * 5 + [vmem] * 2 + [anywhere] * 4,
-        out_specs=(vmem,) * 4,
+        out_specs=(anywhere,) * 4,
         scratch_shapes=[
             tokens, tokens, tokens, tokens, wide,
             pltpu.VMEM(forward.shape, BF16),
@@ -552,7 +561,8 @@
             pltpu.VMEM((X, Z, 8, 1, T), F32),
             pltpu.VMEM((2, Z, W, 1, T), F32),
             pltpu.VMEM((2, 1024), F32),
-            dma((9,)), dma((5, X + 1)), dma((5,)), dma((5, X)), dma((5,)), dma((5,)),
+            pltpu.VMEM((4, T, 1024), BF16),
+            dma((9,)), dma((4,)), dma((5, X + 1)), dma((5,)), dma((5, X)), dma((5,)), dma((5,)),
             dma((6,)), dma((6,)),
             dma((3, 2)), dma((3,)), dma((3,)), dma((3,)), dma((3,)),
         ],

time: 72.2 us -> 72 us (level)
  no operation moved by 1% of the time
where the time goes in v4:
time: 72 us; the launch traced here: 71.8 us
  Pallas kernels  71.2 us (99%)
    pallas_call x1, Pallas kernels, local(): pl.pallas_call(main_kernel, out_shape=(result,) * 4, in_specs=[anywhere]...  69.2 us
    pallas_call x1, Pallas kernels, local(): pl.pallas_call(hand_on_kernel, out_shape=(result,) * 4, in_specs=[anyhow]...  1.98 us

profile of v4, /device:TPU:1, one launch (start us, length us, event | category | flops | bytes accessed | tf_op | source)
XLA Modules:
  0.0 71.8 jit_solution(7959794037642999260)
XLA Ops:
  0.6 69.2 %hyena_exchange.1 = (bf16[128,1024]{1,0:T(8,128)(2,1)}, bf16[128,1024]{1,0:T(8,128)(2,1)}, bf16[128,1024]{1,0:T(8,128)(2,1)}, bf16[128,1024]{1,0:T(8,128)(2,1)}) custom-call(bf16[128,1024]{1,0:T(8,128)(2,1)} %q_hbm.1, bf16[128,1024]{1,0:T(8,128)(2,1)} %k_hbm.1, bf16[128,1024]{1,0:T(8,128)(2,1)} %v_hbm.1, bf16[128,1024]{1,0:T(8,128)(2,1)} %g_hbm.1, ...), custom_call_target="tpu_custom_call" | custom-call | tf_op jit(solution)/shard_map/hyena_exchange/pallas_call | solution.py:531
  69.8 2.0 %hyena_hand_on.1 = (bf16[128,1024]{1,0:T(8,128)(2,1)}, bf16[128,1024]{1,0:T(8,128)(2,1)}, bf16[128,1024]{1,0:T(8,128)(2,1)}, bf16[128,1024]{1,0:T(8,128)(2,1)}) custom-call(bf16[128,1024]{1,0:T(8,128)(2,1)} %get-tuple-element.8.refs_0_, bf16[128,1024]{1,0:T(8,128)(2,1)} %get-tuple-element.9.refs_1_, bf16[128,1024]{1,0:T(8,128)(2,1)} %get-tuple-element.10.refs_2_, ...), custom_call_target="tpu_custom_call" | custom-call | tf_op jit(solution)/shard_map/hyena_hand_on/pallas_call | solution.py:579

commit v5 on v4

--- a/solution.py
+++ b/solution.py
@@ -148,7 +148,7 @@
             body(i)
 
     def columns_of(b):
-        return pl.ds(pl.multiple_of(b * 256, 256), 256)
+        return slice(b * 256, b * 256 + 256)
 
     def pack(p, code):
         def block(b):
@@ -158,7 +158,7 @@
             )
             snd[p, pl.ds(b * 2, 2)] = turned.reshape(2, W, 4, T).astype(BF16)
 
-        each(Z // 2, block)
+        all_of(Z // 2, block)
 
     def send_z(p, source):
         for n, dx in enumerate(ORDER):
@@ -279,7 +279,7 @@
         grad_mixed[:, cols] = value
         tops[1] = jnp.maximum(tops[1], jnp.max(jnp.abs(value).reshape(16, 8, 256), axis=0))
 
-    each(4, gate_block)
+    all_of(4, gate_block)
 
     def top_of(n):
         return jnp.maximum(jnp.max(tops[n], keepdims=True), 1e-30)
@@ -461,19 +461,19 @@
                 + taps[n, 2:3, cols] * extended[n, 2 : T + 2, cols]
             ).astype(BF16)
 
-        each(4, block)
+        all_of(4, block)
         results[n + 1].start()
 
     make_scale_row(0)
     await_all(CONVOLVED)
-    each(4, mix_block)
+    all_of(4, mix_block)
     send_halo(0)
     results[0].start()
     for n in range(X):
         forward(GRAD_GATED, n)
     make_scale_row(1)
     await_all(GRAD_GATED)
-    each(4, grad_block)
+    all_of(4, grad_block)
     send_halo(1)
     send_halo(2)
     await_halo(0)

time: 72 us -> 71.2 us (0.989)
  Pallas kernels: 71.2 us -> 70.2 us
    pallas_call x1, Pallas kernels: 69.2 us -> 68.2 us  [local(): pl.pallas_call(main_kernel, out_shape=(result,) * 4, in_specs=[anywhere]...]
where the time goes in v5:
time: 71.2 us; the launch traced here: 71 us
  Pallas kernels  70.2 us (99%)
  between operations  0.8 us (1%)
    pallas_call x1, Pallas kernels, local(): pl.pallas_call(main_kernel, out_shape=(result,) * 4, in_specs=[anywhere]...  68.2 us
    pallas_call x1, Pallas kernels, local(): pl.pallas_call(hand_on_kernel, out_shape=(result,) * 4, in_specs=[anyhow]...  1.98 us

profile of v5, /device:TPU:1, one launch (start us, length us, event | category | flops | bytes accessed | tf_op | source)
XLA Modules:
  0.0 71.0 jit_solution(10931250693709187926)
XLA Ops:
  0.6 68.2 %hyena_exchange.1 = (bf16[128,1024]{1,0:T(8,128)(2,1)}, bf16[128,1024]{1,0:T(8,128)(2,1)}, bf16[128,1024]{1,0:T(8,128)(2,1)}, bf16[128,1024]{1,0:T(8,128)(2,1)}) custom-call(bf16[128,1024]{1,0:T(8,128)(2,1)} %q_hbm.1, bf16[128,1024]{1,0:T(8,128)(2,1)} %k_hbm.1, bf16[128,1024]{1,0:T(8,128)(2,1)} %v_hbm.1, bf16[128,1024]{1,0:T(8,128)(2,1)} %g_hbm.1, ...), custom_call_target="tpu_custom_call" | custom-call | tf_op jit(solution)/shard_map/hyena_exchange/pallas_call | solution.py:531
  68.9 2.0 %hyena_hand_on.1 = (bf16[128,1024]{1,0:T(8,128)(2,1)}, bf16[128,1024]{1,0:T(8,128)(2,1)}, bf16[128,1024]{1,0:T(8,128)(2,1)}, bf16[128,1024]{1,0:T(8,128)(2,1)}) custom-call(bf16[128,1024]{1,0:T(8,128)(2,1)} %get-tuple-element.8.refs_0_, bf16[128,1024]{1,0:T(8,128)(2,1)} %get-tuple-element.9.refs_1_, bf16[128,1024]{1,0:T(8,128)(2,1)} %get-tuple-element.10.refs_2_, ...), custom_call_target="tpu_custom_call" | custom-call | tf_op jit(solution)/shard_map/hyena_hand_on/pallas_call | solution.py:579
